TPU v7x, 256 devices: a whole 4x4x8 slice. The times are simulated.
256 devices in a mesh: img: 64 (over x, z, core), grp: 4 (over y).
Axes of the slice: x: 4, y: 4, z: 8, core: 2. Of those that a mesh axis runs over, the one named last changes fastest.
Arguments:
- desc: bfloat16 [256, 1024, 256], P(('img', 'grp')), may hold values from -20 to 20
- w_proj: bfloat16 [256, 512], replicated, may hold values from -0.375 to 0.375
- w_out: bfloat16 [256, 256], replicated, may hold values from -0.375 to 0.375
- pair_list: int32 [1280, 2], P(('img', 'grp')), may hold values from 0 to 255, as said below
- pair_count: int32 [256], P(('img', 'grp')), may hold values from 1 to 5, as said below
Outputs:
- updated: bfloat16 [256, 1024, 256], P(('img', 'grp'))
Inputs may be any that keep to these rules, and one draw needn't show every extreme that they name: `pair_list`: for a slot of the device at img index i, the first image lies in column i (ids i * 4 to i * 4 + 3) and the second in column i or column (i + 1) % 64, and the two ids differ; every slot holds such a pair, live or not. `pair_count`: some device has all 5 slots live.
All inputs are finite; a program needn't handle non-finite values.
Results may differ from a plain program's by a relative error of at most 0.0072.
Values may be sent and summed in bfloat16 or wider, within the bound.
No kernel may reach another device: no remote copies, remote signals or barrier semaphores. Data moves between devices by JAX's collectives and lax.ppermute only.
A program may use at most 64 MiB of HBM per device.

v0:
```python
import jax
import jax.numpy as jnp
from jax import lax
from jax.sharding import PartitionSpec as P

D = 256
HEADS = 4
HEAD_DIM = 64


def from_behind(block, axis, distance):
    devices = range(lax.axis_size(axis))
    route = [((i - distance) % len(devices), i) for i in devices]
    return lax.ppermute(block, axis, route)


def pair_messages(first_rows, second_rows):
    to_first = []
    to_second = []
    for head_index in range(HEADS):
        lower = head_index * HEAD_DIM
        query_first = first_rows[:, lower : lower + HEAD_DIM]
        query_second = second_rows[:, lower : lower + HEAD_DIM]
        value_first = first_rows[:, D + lower : D + lower + HEAD_DIM]
        value_second = second_rows[:, D + lower : D + lower + HEAD_DIM]
        scores = jnp.dot(
            query_first, query_second.T, preferred_element_type=jnp.float32
        ) * HEAD_DIM ** (-0.5)
        across = jnp.exp(scores - jnp.max(scores, axis=1, keepdims=True))
        across = (across / jnp.sum(across, axis=1, keepdims=True)).astype(jnp.bfloat16)
        downward = jnp.exp(scores - jnp.max(scores, axis=0, keepdims=True))
        downward = (downward / jnp.sum(downward, axis=0, keepdims=True)).astype(jnp.bfloat16)
        to_first.append(jnp.dot(across, value_second, preferred_element_type=jnp.float32))
        to_second.append(
            lax.dot_general(
                downward, value_first, (((0,), (0,)), ((), ())), preferred_element_type=jnp.float32
            )
        )
    return (
        jnp.concatenate(to_first, 1).astype(jnp.bfloat16),
        jnp.concatenate(to_second, 1).astype(jnp.bfloat16),
    )


def window_slot(image_ids, column_index, columns, members):
    return (image_ids // members - column_index) % columns * members + image_ids % members


def on_device(desc, w_proj, w_out, pair_list, pair_count):
    columns = lax.axis_size("img")
    members = lax.axis_size("grp")
    column_index = lax.axis_index("img")
    keypoints = desc.shape[1]
    own_rows = jnp.dot(desc[0], w_proj, preferred_element_type=jnp.float32).astype(jnp.bfloat16)[
        None
    ]
    group_rows = lax.all_gather(own_rows, "grp", axis=0, tiled=True)
    next_rows = from_behind(group_rows, "img", -1)
    window = jnp.concatenate([group_rows, next_rows], 0)
    live_count = pair_count[0]
    slots = window_slot(pair_list, column_index, columns, members)

    def visit(position, totals):
        first_slot = slots[position, 0]
        second_slot = slots[position, 1]
        first_rows = lax.dynamic_index_in_dim(window, first_slot, 0, keepdims=False)
        second_rows = lax.dynamic_index_in_dim(window, second_slot, 0, keepdims=False)
        to_first, to_second = pair_messages(first_rows, second_rows)
        totals = totals.at[first_slot].add(to_first.astype(jnp.float32))
        return totals.at[second_slot].add(to_second.astype(jnp.float32))

    totals = jnp.zeros((2 * members, keypoints, D), jnp.float32)
    totals = lax.fori_loop(0, live_count, visit, totals)
    returned = from_behind(totals[members:], "img", 1)
    summed = lax.psum_scatter(totals[:members] + returned, "grp", scatter_dimension=0, tiled=True)
    message = summed[0].astype(jnp.bfloat16)
    update = jnp.dot(message, w_out, preferred_element_type=jnp.float32)
    return (desc[0].astype(jnp.float32) + update).astype(jnp.bfloat16)[None]


def solution(mesh):
    return jax.shard_map(
        on_device,
        mesh=mesh,
        in_specs=(
            P(("img", "grp"), None, None),
            P(),
            P(),
            P(("img", "grp"), None),
            P(("img", "grp")),
        ),
        out_specs=P(("img", "grp"), None, None),
        check_vma=False,
    )
```

profile of v0, /device:TPU:1, one launch (start us, length us, event | category | flops | bytes accessed | tf_op | source)
XLA Modules:
  0.0 399.2 jit_solution(12478828602547499768)
XLA Ops:
  7.5 2.5 convolution_convert_fusion
  10.0 54.8 %all-gather.3.cloned.1.call-done = bf16[4096,512]{1,0:T(8,128)(2,1)} async-done(((bf16[1024,512]{1,0:T(8,128)(2,1)}), bf16[4096,512]{1,0:T(8,128)(2,1)}) %all-gather.3.cloned.1.call-update) | async-done | bytes 4194320 | tf_op jit(solution)/shard_map/all_gather | solution.py:57
  66.2 47.0 %collective-permute-done = bf16[4,1024,512]{2,1,0:T(8,128)(2,1)} collective-permute-done((bf16[4,1024,512]{2,1,0:T(8,128)(2,1)}, bf16[4,1024,512]{2,1,0:T(8,128)(2,1)}, u32[]{:S(2)}, u32[]{:S(2)}) %collective-permute-start) | collective-permute-done | bytes 4194336 | tf_op jit(solution)/shard_map/ppermute | solution.py:14
  113.1 7.4 %pad_maximum_fusion = bf16[8,1024,512]{2,1,0:T(8,128)(2,1)} fusion(bf16[4,1024,512]{2,1,0:T(8,128)(2,1)} %collective-permute-done, bf16[4,1024,512]{2,1,0:T(8,128)(2,1)} %bitcast.64), kind=kLoop, calls=%fused_computation.98 | loop fusion | flops 4194304 | bytes 16777216 | tf_op jit(solution)/shard_map/concatenate | solution.py:59
  120.5 4.3 %broadcast_in_dim.6 = f32[8,1024,256]{1,2,0:T(8,128)} broadcast(f32[]{:T(128)} %constant.102.clone.1), dimensions={} | broadcast | bytes 8388612 | tf_op jit(solution)/shard_map/broadcast_in_dim | solution.py:72
  124.8 65.9 %while.12 = (s32[]{:T(128)}, f32[8,1024,256]{1,2,0:T(8,128)}, s32[]{:T(128)}, s32[5,2]{0,1:T(2,128)S(1)}, bf16[8,1024,512]{2,1,0:T(8,128)(2,1)}, /*index=5*/s32[...) while((s32[]{:T(128)}, f32[8,1024,256]{1,2,0:T(8,128)}, s32[]{:T(128)}, ...), condition=%wide.region_19.20_spmd, body=%wide.region_0.19_spmd.sunk | while | flops 1683472384 | bytes 81955088 | solution.py:73
  131.0 1.7 dynamic-slice_bitcast_fusion.3
  133.5 1.6 fusion.108
  142.8 1.6 fusion.104
  147.4 1.6 fusion.102
  151.3 3.0 fusion.110
  154.3 3.1 fusion.115
  163.5 1.7 dynamic-slice_bitcast_fusion.3
  165.9 1.6 fusion.108
  170.6 1.6 fusion.106
  175.2 1.6 fusion.104
  179.9 1.6 fusion.102
  183.7 3.0 fusion.110
  186.8 3.1 fusion.115
  190.8 2.7 slice.93
  193.5 45.4 %collective-permute-done.1 = f32[4,1024,256]{1,2,0:T(8,128)S(1)} collective-permute-done((f32[4,1024,256]{1,2,0:T(8,128)S(1)}, f32[4,1024,256]{1,2,0:T(8,128)S(1)}, u32[]{:S(2)}, u32[]{:S(2)}) %collective-permute-start.1) | collective-permute-done | bytes 4194336 | tf_op jit(solution)/shard_map/ppermute | solution.py:14
  239.0 2.9 slice_add_fusion
  241.8 148.2 %reduce-scatter.2.cloned.1.call-done = f32[1,1024,256]{1,2,0:T(8,128)} async-done(((f32[4,1024,256]{1,2,0:T(8,128)}), f32[1,1024,256]{1,2,0:T(8,128)}) %reduce-scatter.2.cloned.1.call-update) | async-done | bytes 1048592 | tf_op jit(solution)/shard_map/reduce_scatter | solution.py:75
  390.0 2.4 fusion.63
  (46 shorter events, 31.7 us)
Async XLA Ops:
  6.5 1.0 copy-start
  6.5 58.2 %all-gather.3.cloned.1.call-start = ((), (), s32[]{:S(2)}) async-start(), calls=%async_computation.2 | async-start | bytes 5242880 | tf_op jit(solution)/shard_map/all_gather | solution.py:57
  10.0 380.1 %reduce-scatter.2.cloned.1.call-start = ((), (), s32[]{:S(2)}) async-start(), calls=%async_computation.1 | async-start | bytes 5242880 | tf_op jit(solution)/shard_map/reduce_scatter | solution.py:75
  64.8 48.3 %collective-permute-start = (bf16[4,1024,512]{2,1,0:T(8,128)(2,1)}, bf16[4,1024,512]{2,1,0:T(8,128)(2,1)}, u32[]{:S(2)}, u32[]{:S(2)}) collective-permute-start(bf16[4,1024,512]{2,1,0:T(8,128)(2,1)} %bitcast.63), channel_id=1, source_target_pairs={{4,0},{8,4},{12,8},{16,12},{20,16},{24,20},{28,24},{32,28},{36,32}... | collective-permute-start | bytes 12582920 | tf_op jit(solution)/shard_map/ppermute | solution.py:14
  120.5 4.3 %copy-start.4 = (s32[3]{0:T(128)S(1)}, s32[3]{0:T(128)}, u32[]{:S(2)}) copy-start(s32[3]{0:T(128)} %constant.96.clone.1) | copy-start | bytes 40
  190.8 48.2 %copy-start.1 = (f32[8,1024,256]{1,2,0:T(8,128)S(1)}, f32[8,1024,256]{1,2,0:T(8,128)}, u32[]{:S(2)}) copy-start(f32[8,1024,256]{1,2,0:T(8,128)} %get-tuple-element.57) | copy-start | bytes 25165828
  193.4 45.5 %collective-permute-start.1 = (f32[4,1024,256]{1,2,0:T(8,128)S(1)}, f32[4,1024,256]{1,2,0:T(8,128)S(1)}, u32[]{:S(2)}, u32[]{:S(2)}) collective-permute-start(f32[4,1024,256]{1,2,0:T(8,128)S(1)} %slice.93), channel_id=1, source_target_pairs={{252,0},{0,4},{4,8},{8,12},{12,16},{16,20},{20,24},{24,28},{28,32}... | collective-permute-start | bytes 12582920 | tf_op jit(solution)/shard_map/ppermute | solution.py:14
  241.8 148.2 %copy-start.2 = (bf16[1,1024,256]{2,1,0:T(8,128)(2,1)S(1)}, bf16[1,1024,256]{2,1,0:T(8,128)(2,1)}, u32[]{:S(2)}) copy-start(bf16[1,1024,256]{2,1,0:T(8,128)(2,1)} %param.11) | copy-start | bytes 1572868
  241.8 148.2 %copy-start.3 = (bf16[256,256]{1,0:T(8,128)(2,1)S(1)}, bf16[256,256]{1,0:T(8,128)(2,1)}, u32[]{:S(2)}) copy-start(bf16[256,256]{1,0:T(8,128)(2,1)} %param.13) | copy-start | bytes 393220
Sparse Core Ops, SparseCore 0:
  10.1 54.6 all-gather.2
  242.0 148.0 reduce-scatter.1
where the time goes:
time: 400 us; the launch traced here: 399 us
  waiting for transfers between devices  295 us (74%)
  other arithmetic  37.2 us (9%)
  matrix products  29.6 us (7%)
  between operations  13.4 us (3%)
  local copies, waits for them, and re-layouts  12.6 us (3%)
  loops' own time  10.2 us (3%)
    reduce_scatter x1, waiting for transfers between devices, on_device(): lax.psum_scatter(totals[:members] + returned, 'grp', scatter_dimension=0,...  148 us
    ppermute x2, waiting for transfers between devices, from_behind(): return lax.ppermute(block, axis, route)  92.4 us
    all_gather x1, waiting for transfers between devices, on_device(): group_rows = lax.all_gather(own_rows, 'grp', axis=0, tiled=True)  54.8 us
    reduce_sum x8, other arithmetic, pair_messages(): jnp.sum(downward, axis=0, keepdims=True)  12.4 us
    another operation x1, loops' own time, on_device(): totals = lax.fori_loop(0, live_count, visit, totals)  10.2 us
    dot_general x8, matrix products, pair_messages(): jnp.dot(across, value_second, preferred_element_type=jnp.float32)  9.98 us
    dot_general x8, matrix products, pair_messages(): lax.dot_general(downward, value_first, (((0,), (0,)), ((), ())), preferre...  8.13 us
  transfers between devices with their start and end apart: 4, of which 4 were waited for; matrix products, arithmetic and copies ran while one was open for 0% of the time, Pallas kernels for 0%

commit v1 on v0

--- a/solution.py
+++ b/solution.py
@@ -6,6 +6,13 @@
 D = 256
 HEADS = 4
 HEAD_DIM = 64
+
+
+def gather_over(shard, axis, dim):
+    size = lax.axis_size(axis)
+    blocks = jnp.stack([shard for _ in range(size)])
+    blocks = lax.all_to_all(blocks, axis, split_axis=0, concat_axis=0)
+    return jnp.concatenate(blocks, axis=dim)
 
 
 def from_behind(block, axis, distance):
@@ -54,7 +61,7 @@
     own_rows = jnp.dot(desc[0], w_proj, preferred_element_type=jnp.float32).astype(jnp.bfloat16)[
         None
     ]
-    group_rows = lax.all_gather(own_rows, "grp", axis=0, tiled=True)
+    group_rows = gather_over(own_rows, "grp", 0)
     next_rows = from_behind(group_rows, "img", -1)
     window = jnp.concatenate([group_rows, next_rows], 0)
     live_count = pair_count[0]

time: 400 us -> 401 us (level)
  waiting for transfers between devices: 295 us -> 243 us
  blocking collectives: 0 us -> 51.9 us
    all_gather x1 -> x0, waiting for transfers between devices: 54.8 us -> none  [on_device(): group_rows = lax.all_gather(own_rows, 'grp', axis=0, tiled=True)]
    all_to_all x0 -> x1, blocking collectives: none -> 51.9 us  [gather_over(): blocks = lax.all_to_all(blocks, axis, split_axis=0, concat_axis=0)]
  transfers between devices with their start and end apart: 4 -> 3, of which waited for: 4 -> 3; matrix products, arithmetic and copies ran while one was open for 0% -> 0% of each run, Pallas kernels for 0% -> 0%
where the time goes in v1:
time: 401 us; the launch traced here: 399 us
  waiting for transfers between devices  243 us (61%)
  blocking collectives  51.9 us (13%)
  other arithmetic  36.6 us (9%)
  matrix products  28.6 us (7%)
  between operations  13.5 us (3%)
  local copies, waits for them, and re-layouts  12.9 us (3%)
  loops' own time  10.2 us (3%)
    reduce_scatter x1, waiting for transfers between devices, on_device(): lax.psum_scatter(totals[:members] + returned, 'grp', scatter_dimension=0,...  149 us
    ppermute x2, waiting for transfers between devices, from_behind(): return lax.ppermute(block, axis, route)  93.4 us
    all_to_all x1, blocking collectives, gather_over(): blocks = lax.all_to_all(blocks, axis, split_axis=0, concat_axis=0)  51.9 us
    reduce_sum x8, other arithmetic, pair_messages(): jnp.sum(downward, axis=0, keepdims=True)  12.4 us
    another operation x1, loops' own time, on_device(): totals = lax.fori_loop(0, live_count, visit, totals)  10.2 us
    dot_general x8, matrix products, pair_messages(): jnp.dot(across, value_second, preferred_element_type=jnp.float32)  9.99 us
    dot_general x8, matrix products, pair_messages(): lax.dot_general(downward, value_first, (((0,), (0,)), ((), ())), preferre...  8.13 us
  transfers between devices with their start and end apart: 3, of which 3 were waited for; matrix products, arithmetic and copies ran while one was open for 0% of the time, Pallas kernels for 0%

profile of v1, /device:TPU:1, one launch (start us, length us, event | category | flops | bytes accessed | tf_op | source)
XLA Modules:
  0.0 399.3 jit_solution(6498036633131855511)
XLA Ops:
  9.3 51.9 %all_to_all.5 = bf16[4,1,1024,512]{3,2,1,0:T(8,128)(2,1)} all-to-all(bf16[4,1,1024,512]{3,2,1,0:T(8,128)(2,1)S(1)} %stack.3), channel_id=1, replica_groups=mesh['img'=64,'grp'=4] {'grp'}, dimensions={0} | all-to-all | bytes 8388608 | tf_op jit(solution)/shard_map/all_to_all | solution.py:14
  61.2 2.7 collective-permute-start
  64.0 48.0 %collective-permute-done = bf16[4,1024,512]{2,1,0:T(8,128)(2,1)} collective-permute-done((bf16[4,1024,512]{2,1,0:T(8,128)(2,1)}, bf16[4,1024,512]{2,1,0:T(8,128)(2,1)}, u32[]{:S(2)}, u32[]{:S(2)}) %collective-permute-start) | collective-permute-done | bytes 4194336 | tf_op jit(solution)/shard_map/ppermute | solution.py:21
  112.0 7.4 %pad_maximum_fusion = bf16[8,1024,512]{2,1,0:T(8,128)(2,1)} fusion(bf16[4,1024,512]{2,1,0:T(8,128)(2,1)} %collective-permute-done, bf16[4,1024,512]{2,1,0:T(8,128)(2,1)} %bitcast.16), kind=kLoop, calls=%fused_computation.98 | loop fusion | flops 4194304 | bytes 16777216 | tf_op jit(solution)/shard_map/concatenate | solution.py:66
  119.4 4.3 %broadcast_in_dim.4 = f32[8,1024,256]{1,2,0:T(8,128)} broadcast(f32[]{:T(128)} %constant.102.clone.1), dimensions={} | broadcast | bytes 8388612 | tf_op jit(solution)/shard_map/broadcast_in_dim | solution.py:79
  123.7 65.9 %while.12 = (s32[]{:T(128)}, f32[8,1024,256]{1,2,0:T(8,128)}, s32[]{:T(128)}, s32[5,2]{0,1:T(2,128)S(1)}, bf16[8,1024,512]{2,1,0:T(8,128)(2,1)}, /*index=5*/s32[...) while((s32[]{:T(128)}, f32[8,1024,256]{1,2,0:T(8,128)}, s32[]{:T(128)}, ...), condition=%wide.region_19.20_spmd, body=%wide.region_0.19_spmd.sunk | while | flops 1683472384 | bytes 81955088 | solution.py:80
  129.9 1.7 dynamic-slice_bitcast_fusion.3
  132.4 1.6 fusion.108
  137.0 1.6 fusion.106
  141.7 1.6 fusion.104
  146.3 1.6 fusion.102
  150.2 3.0 fusion.110
  153.2 3.1 fusion.115
  162.3 1.7 dynamic-slice_bitcast_fusion.3
  164.8 1.6 fusion.108
  169.5 1.6 fusion.106
  178.8 1.6 fusion.102
  182.6 3.0 fusion.110
  185.7 3.1 fusion.115
  189.6 2.7 slice.93
  192.4 45.4 %collective-permute-done.1 = f32[4,1024,256]{1,2,0:T(8,128)S(1)} collective-permute-done((f32[4,1024,256]{1,2,0:T(8,128)S(1)}, f32[4,1024,256]{1,2,0:T(8,128)S(1)}, u32[]{:S(2)}, u32[]{:S(2)}) %collective-permute-start.1) | collective-permute-done | bytes 4194336 | tf_op jit(solution)/shard_map/ppermute | solution.py:21
  237.8 2.9 slice_add_fusion
  240.7 149.4 %reduce-scatter.2.cloned.1.call-done = f32[1,1024,256]{1,2,0:T(8,128)} async-done(((f32[4,1024,256]{1,2,0:T(8,128)}), f32[1,1024,256]{1,2,0:T(8,128)}) %reduce-scatter.2.cloned.1.call-update) | async-done | bytes 1048592 | tf_op jit(solution)/shard_map/reduce_scatter | solution.py:82
  390.1 2.4 fusion.63
  (47 shorter events, 32.1 us)
Async XLA Ops:
  6.5 1.0 copy-start
  6.5 383.6 %reduce-scatter.2.cloned.1.call-start = ((), (), s32[]{:S(2)}) async-start(), calls=%async_computation.2 | async-start | bytes 5242880 | tf_op jit(solution)/shard_map/reduce_scatter | solution.py:82
  9.3 54.7 %copy-start.5 = (s32[5,2]{0,1:T(2,128)S(1)}, s32[5,2]{0,1:T(2,128)}, u32[]{:S(2)}) copy-start(s32[5,2]{0,1:T(2,128)} %param.14) | copy-start | bytes 124
  61.2 50.8 %collective-permute-start = (bf16[4,1024,512]{2,1,0:T(8,128)(2,1)}, bf16[4,1024,512]{2,1,0:T(8,128)(2,1)}, u32[]{:S(2)}, u32[]{:S(2)}) collective-permute-start(bf16[4,1024,512]{2,1,0:T(8,128)(2,1)} %bitcast.16), channel_id=1, source_target_pairs={{4,0},{8,4},{12,8},{16,12},{20,16},{24,20},{28,24},{32,28},{36,32}... | collective-permute-start | bytes 12582920 | tf_op jit(solution)/shard_map/ppermute | solution.py:21
  119.4 4.3 %copy-start.4 = (s32[3]{0:T(128)S(1)}, s32[3]{0:T(128)}, u32[]{:S(2)}) copy-start(s32[3]{0:T(128)} %constant.96.clone.1) | copy-start | bytes 40
  189.6 48.2 %copy-start.1 = (f32[8,1024,256]{1,2,0:T(8,128)S(1)}, f32[8,1024,256]{1,2,0:T(8,128)}, u32[]{:S(2)}) copy-start(f32[8,1024,256]{1,2,0:T(8,128)} %get-tuple-element.57) | copy-start | bytes 25165828
  192.3 45.5 %collective-permute-start.1 = (f32[4,1024,256]{1,2,0:T(8,128)S(1)}, f32[4,1024,256]{1,2,0:T(8,128)S(1)}, u32[]{:S(2)}, u32[]{:S(2)}) collective-permute-start(f32[4,1024,256]{1,2,0:T(8,128)S(1)} %slice.93), channel_id=1, source_target_pairs={{252,0},{0,4},{4,8},{8,12},{12,16},{16,20},{20,24},{24,28},{28,32}... | collective-permute-start | bytes 12582920 | tf_op jit(solution)/shard_map/ppermute | solution.py:21
  240.7 149.4 %copy-start.2 = (bf16[1,1024,256]{2,1,0:T(8,128)(2,1)S(1)}, bf16[1,1024,256]{2,1,0:T(8,128)(2,1)}, u32[]{:S(2)}) copy-start(bf16[1,1024,256]{2,1,0:T(8,128)(2,1)} %param.11) | copy-start | bytes 1572868
  240.7 149.4 %copy-start.3 = (bf16[256,256]{1,0:T(8,128)(2,1)S(1)}, bf16[256,256]{1,0:T(8,128)(2,1)}, u32[]{:S(2)}) copy-start(bf16[256,256]{1,0:T(8,128)(2,1)} %param.13) | copy-start | bytes 393220
Sparse Core Ops, SparseCore 0:
  240.9 149.2 reduce-scatter.1
